TPU v7x, 256 devices: a whole 4x4x8 slice. The times are simulated.
256 devices in a mesh: wide: 32 (over z, x_hi, core), dp: 8 (over y, x_lo).
Axes of the slice: x: 4 (x_hi: 2, x_lo: 2; x = x_hi * 2 + x_lo), y: 4, z: 8, core: 2. Of those that a mesh axis runs over, the one named last changes fastest.
Arguments:
- queries: bfloat16 [131072, 4096], P(('wide', 'dp')), may hold values from -20 to 20
- teacher_queries: bfloat16 [131072, 4096], P(('wide', 'dp')), may hold values from -6 to 6
- passages: bfloat16 [512, 4096], P('wide'), may hold values from -6 to 6
- bank_student: bfloat16 [8192, 4096], P('wide'), may hold values from -6 to 6
- bank_teacher: bfloat16 [8192, 4096], P('wide'), may hold values from -6 to 6
- owner: int32 [8], P('dp'), may hold values from 0 to 31
- positives: int32 [131072], P(('wide', 'dp')), may hold values from 0 to 511
- keep_mask: int32 [131072, 256], P(('wide', 'dp')), may hold values 0 or 1
Outputs:
- row_loss: float32 [131072], P(('wide', 'dp'))
- query_grad: bfloat16 [131072, 4096], P(('wide', 'dp'))
- passage_grad: float32 [512, 4096], P('wide')
All inputs are finite; a program needn't handle non-finite values. No bound on the sum of `keep_mask` on one device may be relied on, other than what follows from the above.
Results may differ from a plain program's by a relative error of at most 0.0033.
Values may be sent and summed in bfloat16 or wider, within the bound.
A program may use at most 128 MiB of HBM per device.

v0:
```python
import math

import jax
import jax.numpy as jnp
from jax import lax
from jax.sharding import Mesh
from jax.sharding import PartitionSpec as P

E = 4096
WIDE = ("wide_0", "wide_1", "wide_2")
WIDE_DP = ("wide_0", "wide_1", "wide_2", "dp")


def broadcast(block, axis, holder):
    block = jnp.where(lax.axis_index(axis) == holder, block, jnp.zeros_like(block))
    return lax.psum(block, axis)


def laid_out(tiles, dim):
    tiles = jnp.moveaxis(tiles, 0, dim)
    shape = tiles.shape
    return tiles.reshape(*shape[:dim], shape[dim] * shape[dim + 1], *shape[dim + 2 :])


def all_blocks(value, axes, order):
    tiles = value
    for k in order:
        tiles = lax.all_gather(tiles, axes[k])
    done = order[::-1]
    back = [done.index(k) for k in range(len(axes))]
    tiles = tiles.transpose(*back, *range(len(axes), tiles.ndim))
    return tiles.reshape(-1, *value.shape)


def whole_of(value, axes, order, dim):
    return laid_out(all_blocks(value, axes, order), dim)


def own_block(tiles, axes, order):
    shape = [lax.axis_size(a) for a in axes]
    tiles = tiles.reshape(*shape, *tiles.shape[1:])
    tiles = tiles.transpose(*order, *range(len(axes), tiles.ndim))
    tiles = tiles.reshape(-1, *tiles.shape[len(axes) :])
    for k in order:
        tiles = lax.psum_scatter(tiles, axes[k], scatter_dimension=0, tiled=True)
    return tiles[0]


def split_up(value, dim, devices):
    before, after = (value.shape[:dim], value.shape[dim + 1 :])
    return jnp.moveaxis(value.reshape(*before, devices, -1, *after), dim, 0)


def summed_rows_2(value, axes, order, dim):
    devices = lax.axis_size(axes)
    return own_block(split_up(value, dim, devices), axes, order)


def from_everyone(value, axis):
    copies = jnp.broadcast_to(value, (lax.axis_size(axis), *value.shape))
    return lax.all_to_all(copies, axis, split_axis=0, concat_axis=0, tiled=True)


def over_copies(value, axis):
    return from_everyone(value, axis).sum(axis=0)


def body(
    queries, teacher_queries, passages, bank_student, bank_teacher, owner, positives, keep_mask
):
    scale = 2.0 / math.sqrt(E)
    block = passages.shape[0]
    cycle_size = lax.axis_size(WIDE)
    total_rows = block * cycle_size
    pool_s, pool_t = (
        broadcast(bank_student, WIDE, owner[0]),
        broadcast(bank_teacher, WIDE, owner[0]),
    )
    zq = jnp.dot(queries, pool_s.T, preferred_element_type=jnp.float32) * scale
    tt = jnp.dot(teacher_queries, pool_t.T, preferred_element_type=jnp.float32) * scale
    weight = keep_mask.astype(jnp.float32) * jax.nn.sigmoid(-tt)
    pool_top = jnp.max(zq, axis=1)
    pool_total = jnp.sum(weight * jnp.exp(zq - pool_top[:, None]), axis=1)
    piece = whole_of(passages, WIDE, (1, 0, 2), 0)
    run_top = pool_top
    run_total = pool_total
    scores = jnp.dot(queries, piece.T, preferred_element_type=jnp.float32) * scale
    new_top = jnp.maximum(run_top, jnp.max(scores, axis=1))
    run_total = run_total * jnp.exp(run_top - new_top) + jnp.sum(
        jnp.exp(scores - new_top[:, None]), axis=1
    )
    score_store = scores
    passage_store = piece
    run_top, run_total, score_store, passage_store = (
        new_top,
        run_total,
        score_store,
        passage_store,
    )
    lse = run_top + jnp.log(run_total)
    columns = jnp.arange(total_rows, dtype=jnp.int32)
    hit = (columns[None, :] == positives[:, None]).astype(jnp.float32)
    row_loss = lse - jnp.sum(score_store * hit, axis=1)
    grad_p = (jnp.exp(score_store - lse[:, None]) - hit).astype(jnp.bfloat16)
    grad_q = (weight * jnp.exp(zq - lse[:, None])).astype(jnp.bfloat16)
    qgrad = jnp.dot(grad_p, passage_store, preferred_element_type=jnp.float32) + jnp.dot(
        grad_q, pool_s, preferred_element_type=jnp.float32
    )
    local_sums = summed_rows_2(
        lax.dot_general(
            grad_p, queries, (((0,), (0,)), ((), ())), preferred_element_type=jnp.float32
        ),
        WIDE,
        (2, 0, 1),
        0,
    )
    passage_grad = over_copies(local_sums, "dp") * scale
    query_grad = (qgrad * scale).astype(jnp.bfloat16)
    return (row_loss, query_grad, passage_grad)


def solution(mesh):
    torus = Mesh(
        mesh.devices.reshape(8, 2, 2, mesh.shape["dp"]), ("wide_0", "wide_1", "wide_2", "dp")
    )
    in_specs = (
        P(WIDE_DP, None),
        P(WIDE_DP, None),
        P(WIDE, None),
        P(WIDE, None),
        P(WIDE, None),
        P("dp"),
        P(WIDE_DP),
        P(WIDE_DP, None),
    )
    out_specs = (P(WIDE_DP), P(WIDE_DP, None), P(WIDE, None))
    return jax.shard_map(body, mesh=torus, in_specs=in_specs, out_specs=out_specs, check_vma=False)
```

profile of v0, /device:TPU:4, one launch (start us, length us, event | category | flops | bytes accessed | tf_op | source)
XLA Modules:
  0.0 468.3 jit_solution(8938738305149817590)
XLA Ops:
  8.0 0.0 all-gather.6.cloned.1.call-start
  8.0 7.7 %all-gather = bf16[32,4096]{1,0:T(8,128)(2,1)} all-gather(bf16[16,4096]{1,0:T(8,128)(2,1)} %param.10), channel_id=2, replica_groups=mesh['wide_0'=8,'wide_1'=2,'wide_2'=2,'dp'=8] {'wide_1'}, dimensions={0}, use_global_device_ids=true | all-gather | bytes 393216 | tf_op jit(solution)/shard_map/all_gather | solution.py:28
  15.8 0.0 all-gather.6.cloned.1.call-update
  15.8 0.0 all-reduce.3.cloned.1.call-start
  16.5 2.3 broadcast_select_fusion
  18.9 0.0 copy-start.6
  18.9 0.0 all-reduce.3.cloned.1.call-update
  18.9 0.0 all-gather.8.cloned.1.call-start
  18.9 41.1 %all-gather.6.cloned.1.call-done = bf16[16,16,4096]{2,1,0:T(8,128)(2,1)} async-done(((bf16[2,16,4096]{2,1,0:T(8,128)(2,1)}), bf16[16,16,4096]{2,1,0:T(8,128)(2,1)}) %all-gather.6.cloned.1.call-update) | async-done | bytes 2097168 | tf_op jit(solution)/shard_map/all_gather | solution.py:28
  60.0 0.0 all-gather.8.cloned.1.call-update
  60.0 0.0 reduce-scatter.4.cloned.1.call-start
  60.1 0.0 copy-done.6
  60.1 0.2 copy.21
  60.3 241.4 %all-reduce.3.cloned.1.call-done = (bf16[256,4096]{1,0:T(8,128)(2,1)}, bf16[256,4096]{1,0:T(8,128)(2,1)}) async-done(((bf16[256,4096]{1,0:T(8,128)(2,1)}, bf16[256,4096]{1,0:T(8,128)(2,1)}), (bf16[256,4096]{1,0:T(8,128)(2,1)}, bf16[256,4096]{1,0:T(8,128)(2,1)})) %all-reduce.3.cloned.1.call-update) | async-done | bytes 4194320 | tf_op jit(solution)/shard_map/psum | solution.py:16
  301.6 0.0 copy-start.8
  301.6 0.0 copy-start.9
  301.6 4.3 fusion.12
  305.9 0.0 copy-start.3
  305.9 0.8 copy-done.3
  306.7 0.0 copy-done.8
  306.7 0.0 copy-done.9
  306.7 2.2 fusion.6
  309.0 0.0 all-gather.8.cloned.1.call-done
  309.0 0.0 copy-start.1
  309.0 2.6 copy.20
  311.6 0.0 copy-start
  311.6 0.8 copy-done.1
  312.4 0.0 copy-start.7
  312.4 2.4 fusion.13
  314.8 0.0 copy-done
  314.8 0.0 copy-done.7
  314.8 0.3 select_reduce_fusion
  315.1 0.6 fusion.11
  315.7 2.4 fusion.9
  318.1 3.8 copy.22
  321.8 0.0 reduce-scatter.4.cloned.1.call-update
  321.9 0.0 reduce-scatter.6.cloned.1.call-start
  321.9 26.7 %reduce-scatter.4.cloned.1.call-done = f32[16,16,4096]{2,1,0:T(8,128)} async-done(((f32[32,16,4096]{2,1,0:T(8,128)}), f32[16,16,4096]{2,1,0:T(8,128)}) %reduce-scatter.4.cloned.1.call-update) | async-done | bytes 4194320 | tf_op jit(solution)/shard_map/reduce_scatter | solution.py:45
  348.6 0.0 reduce-scatter.6.cloned.1.call-update
  348.6 0.0 reduce-scatter.8.cloned.1.call-start
  348.7 59.1 %reduce-scatter.6.cloned.1.call-done = f32[2,16,4096]{2,1,0:T(8,128)} async-done(((f32[16,16,4096]{2,1,0:T(8,128)}), f32[2,16,4096]{2,1,0:T(8,128)}) %reduce-scatter.6.cloned.1.call-update) | async-done | bytes 524304 | tf_op jit(solution)/shard_map/reduce_scatter | solution.py:45
  407.8 0.0 reduce-scatter.8.cloned.1.call-update
  407.8 17.1 %reduce-scatter.8.cloned.1.call-done = f32[1,16,4096]{2,1,0:T(8,128)} async-done(((f32[2,16,4096]{2,1,0:T(8,128)}), f32[1,16,4096]{2,1,0:T(8,128)}) %reduce-scatter.8.cloned.1.call-update) | async-done | bytes 262160 | tf_op jit(solution)/shard_map/reduce_scatter | solution.py:45
  424.9 2.5 broadcast_in_dim.2
  427.4 6.0 %all-to-all-start = ((f32[8,16,4096]{2,1,0:T(8,128)}), f32[8,16,4096]{2,1,0:T(8,128)S(1)}, u32[]{:S(2)}, u32[]{:S(2)}) async-start(f32[8,16,4096]{2,1,0:T(8,128)} %broadcast_in_dim.2), calls=%async_computation.3 | async-start | bytes 4194304 | tf_op jit(solution)/shard_map/all_to_all | solution.py:61
  433.4 0.0 copy-start.2
  433.4 0.0 copy-start.4
  433.5 0.0 copy-start.5
  433.5 4.8 %fusion.10 = f32[512,4096]{1,0:T(8,128)S(1)} fusion(bf16[512,4096]{1,0:T(8,128)(2,1)} %bitcast.38, f32[512,512]{0,1:T(8,128)S(1)} %get-tuple-element.12, f32[512]{0:T(512)S(1)} %get-tuple-element.8, s32[512]{0:T(512)S(1)} %copy-done.7), kind=kOutput, calls=%fused_computation.22 | convolution fusion | flops 2148794368 | bytes 13635584 | tf_op jit(solution)/shard_map/dot_general | solution.py:106
  438.3 0.0 copy-done.2
  438.3 0.0 copy-done.4
  438.3 0.0 copy-done.5
  438.3 3.4 multiply_convert_fusion
  441.7 18.6 %all-to-all-done = f32[8,16,4096]{2,1,0:T(8,128)S(1)} async-done(((f32[8,16,4096]{2,1,0:T(8,128)}), f32[8,16,4096]{2,1,0:T(8,128)S(1)}, u32[]{:S(2)}, u32[]{:S(2)}) %all-to-all-start) | async-done | bytes 2097184 | tf_op jit(solution)/shard_map/all_to_all | solution.py:61
  460.3 0.1 reduce_sum.39
  460.4 0.7 broadcast_multiply_fusion
  (1 shorter events, 0.0 us)
Async XLA Ops:
  8.0 52.0 %all-gather.6.cloned.1.call-start = ((), (), s32[]{:S(2)}) async-start(), calls=%async_computation.7 | async-start | bytes 2359296 | tf_op jit(solution)/shard_map/all_gather | solution.py:28
  15.8 285.8 %all-reduce.3.cloned.1.call-start = ((), (), s32[]{:S(2)}) async-start(), calls=%async_computation.9 | async-start | bytes 8388608 | tf_op jit(solution)/shard_map/psum | solution.py:16
  18.9 41.2 %copy-start.6 = (s32[512,256]{1,0:T(8,128)S(1)}, s32[512,256]{1,0:T(8,128)}, u32[]{:S(2)}) copy-start(s32[512,256]{1,0:T(8,128)} %param.15) | copy-start | bytes 1572868
  18.9 290.1 %all-gather.8.cloned.1.call-start = ((), (), s32[]{:S(2)}) async-start(), calls=%async_computation.8 | async-start | bytes 6291456 | tf_op jit(solution)/shard_map/all_gather | solution.py:28
  60.0 288.6 %reduce-scatter.4.cloned.1.call-start = ((), (), s32[]{:S(2)}) async-start(), calls=%async_computation.4 | async-start | bytes 12582912 | tf_op jit(solution)/shard_map/reduce_scatter | solution.py:45
  301.6 5.1 %copy-start.8 = (bf16[512,4096]{1,0:T(8,128)(2,1)S(1)}, bf16[512,4096]{1,0:T(8,128)(2,1)}, u32[]{:S(2)}) copy-start(bf16[512,4096]{1,0:T(8,128)(2,1)} %param.9) | copy-start | bytes 12582916
  301.6 5.1 %copy-start.9 = (bf16[256,4096]{1,0:T(8,128)(2,1)S(1)}, bf16[256,4096]{1,0:T(8,128)(2,1)}, u32[]{:S(2)}) copy-start(bf16[256,4096]{1,0:T(8,128)(2,1)} %get-tuple-element.6) | copy-start | bytes 6291460
  305.9 0.8 copy-start.3
  309.0 3.4 copy-start.1
  311.6 3.2 copy-start
  312.4 2.4 copy-start.7
  321.9 85.9 %reduce-scatter.6.cloned.1.call-start = ((), (), s32[]{:S(2)}) async-start(), calls=%async_computation.5 | async-start | bytes 4718592 | tf_op jit(solution)/shard_map/reduce_scatter | solution.py:45
  348.6 76.3 %reduce-scatter.8.cloned.1.call-start = ((), (), s32[]{:S(2)}) async-start(), calls=%async_computation.6 | async-start | bytes 786432 | tf_op jit(solution)/shard_map/reduce_scatter | solution.py:45
  427.4 32.9 %all-to-all-start = ((f32[8,16,4096]{2,1,0:T(8,128)}), f32[8,16,4096]{2,1,0:T(8,128)S(1)}, u32[]{:S(2)}, u32[]{:S(2)}) async-start(f32[8,16,4096]{2,1,0:T(8,128)} %broadcast_in_dim.2), calls=%async_computation.3 | async-start | bytes 4194304 | tf_op jit(solution)/shard_map/all_to_all | solution.py:61
  433.4 4.8 %copy-start.2 = (bf16[256,4096]{1,0:T(8,128)(2,1)S(1)}, bf16[256,4096]{1,0:T(8,128)(2,1)}, u32[]{:S(2)}) copy-start(bf16[256,4096]{1,0:T(8,128)(2,1)} %get-tuple-element.5) | copy-start | bytes 6291460
  433.4 4.9 %copy-start.4 = (f32[256,512]{1,0:T(8,128)S(1)}, f32[256,512]{1,0:T(8,128)}, u32[]{:S(2)}) copy-start(f32[256,512]{1,0:T(8,128)} %copy-done.3) | copy-start | bytes 1572868
  433.5 4.9 %copy-start.5 = (f32[512,256]{0,1:T(8,128)S(1)}, f32[512,256]{0,1:T(8,128)}, u32[]{:S(2)}) copy-start(f32[512,256]{0,1:T(8,128)} %get-tuple-element.14) | copy-start | bytes 1572868
Sparse Core Ops, SparseCore 0:
  15.9 44.0 all-gather.5
  61.8 17.6 all-gather.7
  322.0 26.5 reduce-scatter.3
  351.2 56.5 reduce-scatter.5
Sparse Core Ops, SparseCore 1:
  19.5 282.0 all-reduce.2
  407.9 17.0 reduce-scatter.7
where the time goes:
time: 469 us; the launch traced here: 468 us
  waiting for transfers between devices  404 us (86%)
  matrix products  19.4 us (4%)
  between operations  16 us (3%)
  local copies, waits for them, and re-layouts  10.7 us (2%)
  blocking collectives  7.73 us (2%)
  starting transfers between devices  6.26 us (1%)
    psum x1, waiting for transfers between devices, broadcast(): return lax.psum(block, axis)  241 us
    reduce_scatter x3, waiting for transfers between devices, own_block(): tiles = lax.psum_scatter(tiles, axes[k], scatter_dimension=0, tiled=True)  103 us
    all_gather x2, waiting for transfers between devices, all_blocks(): tiles = lax.all_gather(tiles, axes[k])  41.1 us
    all_to_all x1, waiting for transfers between devices, from_everyone(): return lax.all_to_all(copies, axis, split_axis=0, concat_axis=0, tiled=True)  18.6 us
  transfers between devices with their start and end apart: 7, of which 6 were waited for; matrix products, arithmetic and copies ran while one was open for 4% of the time, Pallas kernels for 0%

commit v1 on v0

--- a/solution.py
+++ b/solution.py
@@ -4,17 +4,152 @@
 import jax.numpy as jnp
 from jax import lax
 from jax.sharding import Mesh
+from jax.experimental import pallas as pl
+from jax.experimental.pallas import tpu as pltpu
 from jax.sharding import PartitionSpec as P
 
 E = 4096
-WIDE = ("wide_0", "wide_1", "wide_2")
-WIDE_DP = ("wide_0", "wide_1", "wide_2", "dp")
-
-
-def broadcast(block, axis, holder):
-    block = jnp.where(lax.axis_index(axis) == holder, block, jnp.zeros_like(block))
-    return lax.psum(block, axis)
-
+WIDE = ("z", "xh", "c")
+DP = ("y", "xl")
+AXES = WIDE + DP
+WIDE_DP = AXES
+MESH = pl.DeviceIdType.MESH
+
+
+def pool_broadcast(PARTS, L):
+    n = PARTS * 16
+    cw = 4096 // PARTS
+    S = n + 15 * L
+
+    def kernel(own_ref, bs, bt, ps, pt, own, oth, R, C, O, lsem, xs, xr, ss, rs, ds, dr):
+        z, xh, c, y, xl = [lax.axis_index(a) for a in AXES]
+        off = 4 * xl
+        q = lax.rem(z - off + 8, 8)
+        p = xh * 7 * 0 + (1 - xh) * q + xh * (15 - q)
+        d = 1 - 2 * c
+        def coords(pp):
+            h = pp // 8
+            qq = (1 - h) * pp + h * (15 - pp)
+            return lax.rem(qq + off, 8), h
+        zn, hn = coords(lax.rem(p + d + 16, 16))
+        zp, hp = coords(lax.rem(p - d + 16, 16))
+        nxt = {"z": zn, "xh": hn}
+        prv = {"z": zp, "xh": hp}
+        peer = {"c": 1 - c}
+        bar = pltpu.get_barrier_semaphore()
+        for dev in (nxt, prv, peer):
+            pl.semaphore_signal(bar, inc=1, device_id=dev, device_id_type=MESH)
+
+        def loads(src):
+            return [pltpu.make_async_copy(src.at[:, pl.ds(i * cw, cw)], own.at[i], lsem.at[i]) for i in range(PARTS)]
+        def xch(src):
+            return [pltpu.make_async_remote_copy(src.at[:, pl.ds(i * cw, cw)], oth.at[i], xs.at[i], xr.at[i], device_id=peer, device_id_type=MESH) for i in range(PARTS)]
+
+        @pl.when(c == 0)
+        def _():
+            for k in loads(bs): k.start()
+        @pl.when(c == 1)
+        def _():
+            for k in loads(bt): k.start()
+        pl.semaphore_wait(bar, 3)
+        @pl.when(c == 0)
+        def _():
+            for k in xch(bt): k.start()
+        @pl.when(c == 1)
+        def _():
+            for k in xch(bs): k.start()
+
+        o = own_ref[0]
+        oz, oh, oc = o // 4, lax.rem(o // 2, 2), lax.rem(o, 2)
+        oq = lax.rem(oz - off + 8, 8)
+        op = (1 - oh) * oq + oh * (15 - oq)
+        mine = jnp.logical_and(op == p, oc == c)
+        other = jnp.logical_and(op == p, oc == 1 - c)
+        fv = lax.rem(p - op + 16, 16)
+        bv = lax.rem(op - p + 16, 16)
+        v = jnp.where(c == 0, fv, bv)
+        vo = jnp.where(c == 0, bv, fv)
+
+        def ring(s):
+            return pltpu.make_async_remote_copy(C.at[s], R.at[s], ss.at[s], rs.at[s], device_id=nxt, device_id_type=MESH)
+        def d2d(s):
+            return pltpu.make_async_remote_copy(C.at[s], O.at[s], ds.at[s], dr.at[s], device_id=peer, device_id_type=MESH)
+        def inj(s):
+            part = s // 16
+            rows = pl.ds(pl.multiple_of(lax.rem(s, 16) * 16, 16), 16)
+            return own[part, rows, :], oth[part, rows, :]
+        def waitx(i):
+            pltpu.make_async_copy(own.at[i], own.at[i], lsem.at[i]).wait()
+            pltpu.make_async_remote_copy(oth.at[i], oth.at[i], xs.at[i], xr.at[i], device_id=peer, device_id_type=MESH).wait()
+        assert L <= 16
+        for i in range(PARTS):
+            waitx(i)
+            def body1(s, _):
+                a, b = inj(s)
+                C[s] = jnp.where(mine, a, b)
+                ring(s).start(); d2d(s).start()
+                return 0
+            def body2(s, _):
+                a, b = inj(s)
+                ring(s - L).wait_recv()
+                C[s] = jnp.where(mine, a, jnp.where(other, b, R[s - L]))
+                ring(s).start(); d2d(s).start()
+                return 0
+            lo = 16 * i
+            if i == 0:
+                lax.fori_loop(0, L, body1, 0)
+                lo = L
+            lax.fori_loop(lo, 16 * i + 16, body2, 0)
+        def body3(s, _):
+            ring(s - L).wait_recv()
+            C[s] = R[s - L]
+            ring(s).start(); d2d(s).start()
+            return 0
+        lax.fori_loop(n, S - L, body3, 0)
+        def body4(s, _):
+            ring(s - L).wait_recv()
+            C[s] = R[s - L]
+            d2d(s).start()
+            return 0
+        lax.fori_loop(S - L, S, body4, 0)
+        def fin(s, _):
+            ring(s).wait_send()
+            return 0
+        lax.fori_loop(0, S - L, fin, 0)
+        def fin2(s, _):
+            d2d(s).wait()
+            return 0
+        lax.fori_loop(0, S, fin2, 0)
+        for i in range(PARTS):
+            A = C[pl.ds(v * L + 16 * i, 16)].reshape(256, cw)
+            B = O[pl.ds(vo * L + 16 * i, 16)].reshape(256, cw)
+            ps[:, pl.ds(i * cw, cw)] = jnp.where(c == 0, A, B)
+            pt[:, pl.ds(i * cw, cw)] = jnp.where(c == 0, B, A)
+
+    def call(owner, bs, bt):
+        return pl.pallas_call(
+            kernel,
+            out_shape=[jax.ShapeDtypeStruct((256, 4096), jnp.bfloat16)] * 2,
+            in_specs=[pl.BlockSpec(memory_space=pltpu.SMEM), pl.BlockSpec(memory_space=pl.ANY), pl.BlockSpec(memory_space=pl.ANY)],
+            out_specs=[pl.BlockSpec(memory_space=pltpu.VMEM)] * 2,
+            scratch_shapes=[
+                pltpu.VMEM((PARTS, 256, cw), jnp.bfloat16),
+                pltpu.VMEM((PARTS, 256, cw), jnp.bfloat16),
+                pltpu.VMEM((S - L, 16, cw), jnp.bfloat16),
+                pltpu.VMEM((S, 16, cw), jnp.bfloat16),
+                pltpu.VMEM((S, 16, cw), jnp.bfloat16),
+                pltpu.SemaphoreType.DMA((PARTS,)),
+                pltpu.SemaphoreType.DMA((PARTS,)),
+                pltpu.SemaphoreType.DMA((PARTS,)),
+                pltpu.SemaphoreType.DMA((S - L,)),
+                pltpu.SemaphoreType.DMA((S - L,)),
+                pltpu.SemaphoreType.DMA((S,)),
+                pltpu.SemaphoreType.DMA((S,)),
+            ],
+            compiler_params=pltpu.CompilerParams(collective_id=0, has_side_effects=True, vmem_limit_bytes=48 << 20),
+            name=f"pool_{PARTS}_{L}",
+        )(owner, bs, bt)
+    return call
 
 def laid_out(tiles, dim):
     tiles = jnp.moveaxis(tiles, 0, dim)
@@ -72,10 +207,7 @@
     block = passages.shape[0]
     cycle_size = lax.axis_size(WIDE)
     total_rows = block * cycle_size
-    pool_s, pool_t = (
-        broadcast(bank_student, WIDE, owner[0]),
-        broadcast(bank_teacher, WIDE, owner[0]),
-    )
+    pool_s, pool_t = pool_broadcast(4, 8)(owner, bank_student, bank_teacher)
     zq = jnp.dot(queries, pool_s.T, preferred_element_type=jnp.float32) * scale
     tt = jnp.dot(teacher_queries, pool_t.T, preferred_element_type=jnp.float32) * scale
     weight = keep_mask.astype(jnp.float32) * jax.nn.sigmoid(-tt)
@@ -114,14 +246,14 @@
         (2, 0, 1),
         0,
     )
-    passage_grad = over_copies(local_sums, "dp") * scale
+    passage_grad = over_copies(local_sums, DP) * scale
     query_grad = (qgrad * scale).astype(jnp.bfloat16)
     return (row_loss, query_grad, passage_grad)
 
 
 def solution(mesh):
     torus = Mesh(
-        mesh.devices.reshape(8, 2, 2, mesh.shape["dp"]), ("wide_0", "wide_1", "wide_2", "dp")
+        mesh.devices.reshape(8, 2, 2, 4, 2), AXES
     )
     in_specs = (
         P(WIDE_DP, None),
@@ -129,7 +261,7 @@
         P(WIDE, None),
         P(WIDE, None),
         P(WIDE, None),
-        P("dp"),
+        P(DP),
         P(WIDE_DP),
         P(WIDE_DP, None),
     )

time: 469 us -> 307 us (0.65)
  waiting for transfers between devices: 404 us -> 163 us
  Pallas kernels: 0 us -> 83.3 us
    psum x1 -> x0, waiting for transfers between devices: 241 us -> none  [broadcast(): return lax.psum(block, axis)]
    pallas_call x0 -> x1, Pallas kernels: none -> 83.3 us  [call(): pl.pallas_call(kernel, out_shape=[jax.ShapeDtypeStruct((256, 4096), jnp.b...]
  transfers between devices with their start and end apart: 7 -> 6, of which waited for: 6 -> 5; matrix products, arithmetic and copies ran while one was open for 4% -> 4% of each run, Pallas kernels for 0% -> 27%
where the time goes in v1:
time: 307 us; the launch traced here: 306 us
  waiting for transfers between devices  163 us (53%)
  Pallas kernels  83.3 us (27%)
  matrix products  16.4 us (5%)
  between operations  14.6 us (5%)
  local copies, waits for them, and re-layouts  11.8 us (4%)
  blocking collectives  7.73 us (3%)
  starting transfers between devices  6.24 us (2%)
  other arithmetic  3.34 us (1%)
    reduce_scatter x3, waiting for transfers between devices, own_block(): tiles = lax.psum_scatter(tiles, axes[k], scatter_dimension=0, tiled=True)  99.5 us
    pallas_call x1, Pallas kernels, call(): pl.pallas_call(kernel, out_shape=[jax.ShapeDtypeStruct((256, 4096), jnp.b...  83.3 us
    all_gather x2, waiting for transfers between devices, all_blocks(): tiles = lax.all_gather(tiles, axes[k])  44.2 us
    all_to_all x1, waiting for transfers between devices, from_everyone(): return lax.all_to_all(copies, axis, split_axis=0, concat_axis=0, tiled=True)  18.9 us
    all_gather x1, blocking collectives, all_blocks(): tiles = lax.all_gather(tiles, axes[k])  7.73 us
  transfers between devices with their start and end apart: 6, of which 5 were waited for; matrix products, arithmetic and copies ran while one was open for 4% of the time, Pallas kernels for 27%

profile of v1, /device:TPU:4, one launch (start us, length us, event | category | flops | bytes accessed | tf_op | source)
XLA Modules:
  0.0 306.0 jit_solution(16279156342470835809)
XLA Ops:
  7.2 0.0 all-gather.6.cloned.1.call-start
  7.2 7.7 %all-gather = bf16[32,4096]{1,0:T(8,128)(2,1)} all-gather(bf16[16,4096]{1,0:T(8,128)(2,1)} %param.10), channel_id=2, replica_groups=mesh['z'=8,'xh'=2,'c'=2,'y'=4,'xl'=2] {'xh'}, dimensions={0}, use_global_device_ids=true | all-gather | bytes 393216 | tf_op jit(solution)/shard_map/all_gather | solution.py:163
  14.9 0.0 all-gather.6.cloned.1.call-update
  15.0 0.0 all-gather.8.cloned.1.call-start
  15.0 44.1 %all-gather.6.cloned.1.call-done = bf16[16,16,4096]{2,1,0:T(8,128)(2,1)} async-done(((bf16[2,16,4096]{2,1,0:T(8,128)(2,1)}), bf16[16,16,4096]{2,1,0:T(8,128)(2,1)}) %all-gather.6.cloned.1.call-update) | async-done | bytes 2097168 | tf_op jit(solution)/shard_map/all_gather | solution.py:163
  59.2 0.0 all-gather.8.cloned.1.call-update
  59.2 0.0 reduce-scatter.4.cloned.1.call-start
  59.9 1.2 copy.21
  61.1 0.0 copy-start.1
  61.1 83.3 %pool_4_8.1 = (bf16[256,4096]{1,0:T(8,128)(2,1)S(1)}, bf16[256,4096]{1,0:T(8,128)(2,1)S(1)}) custom-call(s32[1]{0:T(128)S(6)} %copy.23.own_ref, bf16[256,4096]{1,0:T(8,128)(2,1)} %bs.1, bf16[256,4096]{1,0:T(8,128)(2,1)} %bt.1), custom_call_target="tpu_custom_call" | custom-call | tf_op jit(solution)/shard_map/pool_4_8/pallas_call | solution.py:130
  144.4 0.0 copy-start.7
  144.4 0.0 copy-done.1
  144.5 1.3 fusion.12
  145.8 0.0 copy-start.3
  145.8 0.8 copy-done.3
  146.6 0.0 copy-done.7
  146.6 2.2 fusion.6
  148.9 0.0 all-gather.8.cloned.1.call-done
  148.9 0.0 copy-start.2
  148.9 2.6 copy.20
  151.5 0.0 copy-start
  151.5 0.8 copy-done.2
  152.3 0.0 copy-start.6
  152.3 2.4 fusion.13
  154.7 0.0 copy-done
  154.7 0.0 copy-done.6
  154.7 0.3 select_reduce_fusion
  155.0 0.6 fusion.11
  155.6 2.4 fusion.9
  158.0 3.8 %copy.22 = f32[8,2,2,16,4096]{4,3,1,0,2:T(8,128)} copy(f32[8,2,2,16,4096]{4,3,2,1,0:T(8,128)S(1)} %bitcast.34) | data formatting | bytes 16777216 | tf_op jit(solution)/shard_map/reshape;reshape | solution.py:176
  161.7 0.0 reduce-scatter.4.cloned.1.call-update
  161.8 0.0 reduce-scatter.6.cloned.1.call-start
  161.8 20.8 %reduce-scatter.4.cloned.1.call-done = f32[16,16,4096]{2,1,0:T(8,128)} async-done(((f32[32,16,4096]{2,1,0:T(8,128)}), f32[16,16,4096]{2,1,0:T(8,128)}) %reduce-scatter.4.cloned.1.call-update) | async-done | bytes 4194320 | tf_op jit(solution)/shard_map/reduce_scatter | solution.py:180
  182.6 0.0 reduce-scatter.6.cloned.1.call-update
  182.6 0.0 reduce-scatter.8.cloned.1.call-start
  182.6 59.1 %reduce-scatter.6.cloned.1.call-done = f32[2,16,4096]{2,1,0:T(8,128)} async-done(((f32[16,16,4096]{2,1,0:T(8,128)}), f32[2,16,4096]{2,1,0:T(8,128)}) %reduce-scatter.6.cloned.1.call-update) | async-done | bytes 524304 | tf_op jit(solution)/shard_map/reduce_scatter | solution.py:180
  241.7 0.0 reduce-scatter.8.cloned.1.call-update
  241.8 19.6 %reduce-scatter.8.cloned.1.call-done = f32[1,16,4096]{2,1,0:T(8,128)} async-done(((f32[2,16,4096]{2,1,0:T(8,128)}), f32[1,16,4096]{2,1,0:T(8,128)}) %reduce-scatter.8.cloned.1.call-update) | async-done | bytes 262160 | tf_op jit(solution)/shard_map/reduce_scatter | solution.py:180
  261.4 2.5 broadcast_in_dim.2
  263.9 6.0 %all-to-all-start = ((f32[8,16,4096]{2,1,0:T(8,128)}), f32[8,16,4096]{2,1,0:T(8,128)}, u32[]{:S(2)}, u32[]{:S(2)}) async-start(f32[8,16,4096]{2,1,0:T(8,128)} %broadcast_in_dim.2), calls=%async_computation.3 | async-start | bytes 4194304 | tf_op jit(solution)/shard_map/all_to_all | solution.py:196
  269.9 0.0 copy-start.4
  269.9 0.0 copy-start.5
  269.9 4.8 %fusion.10 = f32[512,4096]{1,0:T(8,128)S(1)} fusion(bf16[512,4096]{1,0:T(8,128)(2,1)} %bitcast.36, f32[512,512]{0,1:T(8,128)S(1)} %get-tuple-element.14, f32[512]{0:T(512)S(1)} %get-tuple-element.10, s32[512]{0:T(512)S(1)} %copy-done.6), kind=kOutput, calls=%fused_computation.20 | convolution fusion | flops 2148794368 | bytes 13635584 | tf_op jit(solution)/shard_map/dot_general | solution.py:238
  274.7 0.0 copy-done.4
  274.7 0.0 copy-done.5
  274.7 3.4 %multiply_convert_fusion = bf16[512,4096]{1,0:T(8,128)(2,1)} fusion(f32[512,4096]{1,0:T(8,128)S(1)} %fusion.10, bf16[256,4096]{1,0:T(8,128)(2,1)S(1)} %get-tuple-element.5, f32[512,256]{0,1:T(8,128)S(1)} %copy-done.5, f32[256,512]{1,0:T(8,128)S(1)} %copy-done.4, f32[512]{0:T(512)S(1)} %get-tuple-element.10), kind=kOutput, calls=%fused_computation | convolution fusion | flops 1080426496 | bytes 15730688 | tf_op jit(solution)/shard_map/dot_general | solution.py:238
  278.1 18.9 %all-to-all-done = f32[8,16,4096]{2,1,0:T(8,128)} async-done(((f32[8,16,4096]{2,1,0:T(8,128)}), f32[8,16,4096]{2,1,0:T(8,128)}, u32[]{:S(2)}, u32[]{:S(2)}) %all-to-all-start) | async-done | bytes 2097184 | tf_op jit(solution)/shard_map/all_to_all | solution.py:196
  297.0 1.7 reduce_sum.39
  298.7 0.7 broadcast_multiply_fusion
  (1 shorter events, 0.0 us)
Async XLA Ops:
  7.2 52.0 %all-gather.6.cloned.1.call-start = ((), (), s32[]{:S(2)}) async-start(), calls=%async_computation.7 | async-start | bytes 2359296 | tf_op jit(solution)/shard_map/all_gather | solution.py:163
  15.0 133.9 %all-gather.8.cloned.1.call-start = ((), (), s32[]{:S(2)}) async-start(), calls=%async_computation.8 | async-start | bytes 6291456 | tf_op jit(solution)/shard_map/all_gather | solution.py:163
  59.2 123.4 %reduce-scatter.4.cloned.1.call-start = ((), (), s32[]{:S(2)}) async-start(), calls=%async_computation.4 | async-start | bytes 12582912 | tf_op jit(solution)/shard_map/reduce_scatter | solution.py:180
  61.1 83.3 %copy-start.1 = (bf16[512,4096]{1,0:T(8,128)(2,1)S(1)}, bf16[512,4096]{1,0:T(8,128)(2,1)}, u32[]{:S(2)}) copy-start(bf16[512,4096]{1,0:T(8,128)(2,1)} %param.8) | copy-start | bytes 12582916
  144.4 2.2 copy-start.7
  145.8 0.8 copy-start.3
  148.9 3.4 %copy-start.2 = (bf16[512,4096]{1,0:T(8,128)(2,1)S(1)}, bf16[512,4096]{1,0:T(8,128)(2,1)}, u32[]{:S(2)}) copy-start(bf16[512,4096]{1,0:T(8,128)(2,1)} %param.8) | copy-start | bytes 12582916
  151.5 3.2 %copy-start = (bf16[8,2,2,16,4096]{4,3,2,1,0:T(8,128)(2,1)}, bf16[8,2,2,16,4096]{4,3,2,1,0:T(8,128)(2,1)S(1)}, u32[]{:S(2)}) copy-start(bf16[8,2,2,16,4096]{4,3,2,1,0:T(8,128)(2,1)S(1)} %copy.20) | copy-start | bytes 12582916
  152.3 2.4 copy-start.6
  161.8 80.0 %reduce-scatter.6.cloned.1.call-start = ((), (), s32[]{:S(2)}) async-start(), calls=%async_computation.5 | async-start | bytes 4718592 | tf_op jit(solution)/shard_map/reduce_scatter | solution.py:180
  182.6 78.8 %reduce-scatter.8.cloned.1.call-start = ((), (), s32[]{:S(2)}) async-start(), calls=%async_computation.6 | async-start | bytes 786432 | tf_op jit(solution)/shard_map/reduce_scatter | solution.py:180
  263.9 33.1 %all-to-all-start = ((f32[8,16,4096]{2,1,0:T(8,128)}), f32[8,16,4096]{2,1,0:T(8,128)}, u32[]{:S(2)}, u32[]{:S(2)}) async-start(f32[8,16,4096]{2,1,0:T(8,128)} %broadcast_in_dim.2), calls=%async_computation.3 | async-start | bytes 4194304 | tf_op jit(solution)/shard_map/all_to_all | solution.py:196
  269.9 4.8 %copy-start.4 = (f32[256,512]{1,0:T(8,128)S(1)}, f32[256,512]{1,0:T(8,128)}, u32[]{:S(2)}) copy-start(f32[256,512]{1,0:T(8,128)} %copy-done.3) | copy-start | bytes 1572868
  269.9 4.8 %copy-start.5 = (f32[512,256]{0,1:T(8,128)S(1)}, f32[512,256]{0,1:T(8,128)}, u32[]{:S(2)}) copy-start(f32[512,256]{0,1:T(8,128)} %get-tuple-element.16) | copy-start | bytes 1572868
Sparse Core Ops, SparseCore 0:
  15.1 44.0 all-gather.5
  61.0 17.8 all-gather.7
  161.9 20.6 reduce-scatter.3
  185.1 56.5 reduce-scatter.5
  244.2 17.0 reduce-scatter.7

commit v2 on v0

v2 whole, which is shorter than its diff:
```python
import math

import jax
import jax.numpy as jnp
from jax import lax
from jax.experimental import pallas as pl
from jax.experimental.pallas import tpu as pltpu
from jax.sharding import Mesh
from jax.sharding import PartitionSpec as P

E = 4096
WIDE = ("z", "xh", "c")
DP = ("y", "xl")
AXES = WIDE + DP
MESH = pl.DeviceIdType.MESH
SCALE = 2.0 / math.sqrt(E)
BF = jnp.bfloat16
F32 = jnp.float32

PARTS = 4
CW = E // PARTS
N = PARTS * 16
L = 8
L2 = 12
S = N + 8 * L + L2
BATCH = 4
NB = S // BATCH
assert S % BATCH == 0
EDGES = sorted({0, L, L2, N, N + L, N + L + L2, S - L, S} | {16 * i for i in range(PARTS)})

NT = (((1,), (1,)), ((), ()))


def dot(a, b):
    return jnp.dot(a, b, preferred_element_type=F32)


def dot_nt(a, b):
    return lax.dot_general(a, b, NT, preferred_element_type=F32)


def kernel(
    owner_ref, q_hbm, t_hbm, p_hbm, bs_hbm, bt_hbm, pos_ref, keep_ref,
    loss_ref, qg_hbm, pg_ref,
    q, t, pa, own, oth, ring_in, rung_in, stream,
    zp_t, zq_t, tt_t, gp_t, gp, gq,
    give, got, kept, merged, first_y, first_x, second_out, second_in, piece, third_in,
    load_sem, own_sem, oth_s, oth_r, ring_s, ring_r, rung_s, rung_r, share_s, share_r,
    pz_s, pz_r, px_s, px_r, py_s, py_r, pc_s, pc_r,
    gc_s, gc_r, g1_s, g1_r, g2_s, g2_r, g3_s, g3_r, g4_s, g4_r, out_sem,
):
    z, xh, c, y, xl = [lax.axis_index(a) for a in AXES]
    x = xh * 2 + xl

    def along_x(j):
        other = lax.rem(x + j, 4)
        return {"xh": other // 2, "xl": lax.rem(other, 2)}

    zs = {j: {"z": lax.rem(z + j, 8)} for j in range(1, 8)}
    xs = {j: along_x(j) for j in range(1, 4)}
    ys = {j: {"y": lax.rem(y + j, 4)} for j in range(1, 4)}
    peer = {"c": 1 - c}
    dps = {
        2 * a + b: {"y": lax.rem(y + a, 4), "xl": lax.rem(xl + b, 2)}
        for a in range(4)
        for b in range(2)
        if a or b
    }

    def send(src, dst, send_sem, recv_sem, device):
        return pltpu.make_async_remote_copy(
            src, dst, send_sem, recv_sem, device_id=device, device_id_type=MESH
        )

    barrier = pltpu.get_barrier_semaphore()
    greeted = [*zs.values(), *xs.values(), peer, *[dps[k] for k in dps if k != 1]]
    for device in greeted:
        pl.semaphore_signal(barrier, inc=1, device_id=device, device_id_type=MESH)

    pcol = pl.multiple_of(y * 1024 + xl * 512, 512)
    prow = pl.multiple_of(xh * 128 + z * 16, 16)
    mine_p = pa.at[c, pl.ds(prow, 16), pl.ds(pcol, 512)]
    load_p = pltpu.make_async_copy(p_hbm.at[:, pl.ds(pcol, 512)], mine_p, load_sem.at[2])
    load_p.start()

    def own_loads(src):
        return [
            pltpu.make_async_copy(src.at[:, pl.ds(i * CW, CW)], own.at[i], own_sem.at[i])
            for i in range(PARTS)
        ]

    def other_loads(src):
        return [
            send(src.at[:, pl.ds(i * CW, CW)], oth.at[i], oth_s.at[i], oth_r.at[i], peer)
            for i in range(PARTS)
        ]

    @pl.when(c == 0)
    def _():
        for k in own_loads(bs_hbm):
            k.start()

    @pl.when(c == 1)
    def _():
        for k in own_loads(bt_hbm):
            k.start()

    load_q = pltpu.make_async_copy(q_hbm, q, load_sem.at[0])
    load_t = pltpu.make_async_copy(t_hbm, t, load_sem.at[1])
    pl.semaphore_wait(barrier, len(greeted))

    @pl.when(c == 0)
    def _():
        for k in other_loads(bt_hbm):
            k.start()

    @pl.when(c == 1)
    def _():
        for k in other_loads(bs_hbm):
            k.start()

    load_p.wait()
    pz = {j: send(mine_p, mine_p, pz_s.at[j], pz_r.at[j], zs[j]) for j in zs}
    half = pa.at[c, pl.ds(pl.multiple_of(xh * 128, 128), 128), pl.ds(pcol, 512)]
    px = {j: send(half, half, px_s.at[j], px_r.at[j], xs[j]) for j in xs}
    quarter = pa.at[c, :, pl.ds(pl.multiple_of(y * 1024, 1024), 1024)]
    py = {j: send(quarter, quarter, py_s.at[j], py_r.at[j], ys[j]) for j in ys}
    pc = send(pa.at[c], pa.at[c], pc_s, pc_r, peer)
    for j in pz:
        pz[j].start()

    o = owner_ref[0]
    oz, oh, oc = o // 4, lax.rem(o // 2, 2), lax.rem(o, 2)
    here = jnp.logical_and(oz == z, oh == xh)
    mine = jnp.logical_and(here, oc == c)
    other = jnp.logical_and(here, oc == 1 - c)

    def place(core):
        v = lax.rem((z - oz) * (1 - 2 * core) + 8, 8)
        e = lax.rem(oz + xl + core, 2)
        across = (e + lax.rem(v - e + 8, 8)) * L + L2
        return v, e, jnp.where(oh == xh, v * L, across)

    dist = lax.rem((z - oz) * (1 - 2 * c) + 8, 8)
    enter = lax.rem(oz + xl + c, 2)
    use_rung = jnp.logical_and(oh != xh, dist == enter)
    rung = lax.rem(z + xl + c, 2) == 0
    nxt = {"z": lax.rem(z + 9 - 2 * c, 8)}

    def ring(s):
        return send(stream.at[c, s], ring_in.at[s], ring_s.at[s], ring_r.at[s], nxt)

    def cross(s):
        return send(stream.at[c, s], rung_in.at[s], rung_s.at[s], rung_r.at[s], {"xh": 1 - xh})

    def share(b):
        block = stream.at[c, pl.ds(b * BATCH, BATCH)]
        return send(block, block, share_s.at[b], share_r.at[b], peer)

    def step(s, lo):
        from_ring, injecting = lo >= L, lo < N
        from_rung = L2 <= lo < N + L + L2
        if injecting:
            rows = pl.ds(pl.multiple_of(lax.rem(s, 16) * 16, 16), 16)
        if from_ring:
            ring(s - L).wait_recv()

        def content(with_rung):
            value = None
            if from_ring:
                value = ring_in[s - L]
            if with_rung:
                value = jnp.where(use_rung, rung_in[s - L2], value)
            if injecting:
                a, b = own[s // 16, rows, :], oth[s // 16, rows, :]
                rest = b if value is None else jnp.where(other, b, value)
                value = jnp.where(mine, a, rest)
            return value

        if from_rung:

            @pl.when(rung)
            def _():
                cross(s - L2).wait_recv()
                stream[c, s] = content(True)

            @pl.when(jnp.logical_not(rung))
            def _():
                stream[c, s] = content(False)

        else:
            stream[c, s] = content(False)
        if lo < S - L:
            ring(s).start()
        if lo < N + L:

            @pl.when(rung)
            def _():
                cross(s).start()

        @pl.when(lax.rem(s, BATCH) == BATCH - 1)
        def _():
            share(s // BATCH).start()

    def run(a, b):
        cuts = [a] + [k for k in EDGES if a < k < b] + [b]
        for lo, hi in zip(cuts[:-1], cuts[1:]):
            if lo < N and lo % 16 == 0:
                pltpu.make_async_copy(own.at[lo // 16], own.at[lo // 16], own_sem.at[lo // 16]).wait()
                k = lo // 16
                send(oth.at[k], oth.at[k], oth_s.at[k], oth_r.at[k], peer).wait()

            def body(s, carry, lo=lo):
                step(s, lo)
                return carry

            lax.fori_loop(lo, hi, body, 0)

    run(0, 24)
    load_q.start()
    load_t.start()
    for j in pz:
        pz[j].wait_recv()
    for j in px:
        px[j].start()
    run(24, 40)
    for j in px:
        px[j].wait_recv()
    for j in py:
        py[j].start()
    run(40, 116)
    for j in py:
        py[j].wait_recv()
    pc.start()
    run(116, S)
    load_q.wait()
    load_t.wait()
    pc.wait_recv()

    for h in range(2):
        zp_t[pl.ds(h * 256, 256), :] = dot_nt(pa[h], q[...]) * SCALE

    def got_share(b, carry):
        share(b).wait_recv()
        return carry

    lax.fori_loop(0, NB, got_share, 0)
    _, _, at_s = place(0)
    _, _, at_t = place(1)

    def bank(core, at, i):
        return stream[core, pl.ds(at + 16 * i, 16)].reshape(256, CW)

    for target, core, at, left in ((zq_t, 0, at_s, q), (tt_t, 1, at_t, t)):
        for i in range(PARTS):
            part = dot_nt(bank(core, at, i), left[:, pl.ds(i * CW, CW)])
            target[...] = part if i == 0 else target[...] + part
    zq = zq_t[...] * SCALE
    weight = jnp.transpose(keep_ref[...].astype(F32)) * jax.nn.sigmoid(-(tt_t[...] * SCALE))
    zp = zp_t[...]
    top = jnp.maximum(jnp.max(zp, axis=0, keepdims=True), jnp.max(zq, axis=0, keepdims=True))
    total = jnp.sum(jnp.exp(zp - top), axis=0, keepdims=True) + jnp.sum(
        weight * jnp.exp(zq - top), axis=0, keepdims=True
    )
    lse = top + jnp.log(total)
    k = lax.broadcasted_iota(jnp.int32, (512, 512), 0)
    ids = (lax.rem(k // 16, 8) * 4 + lax.rem(k // 128, 2) * 2 + k // 256) * 16 + lax.rem(k, 16)
    hit = (ids == pos_ref[...]).astype(F32)
    loss_ref[...] = lse - jnp.sum(zp * hit, axis=0, keepdims=True)
    grad = jnp.exp(zp - lse) - hit
    gp_t[...] = grad.astype(BF)
    gp[...] = jnp.transpose(grad).astype(BF)
    gq[...] = jnp.transpose(weight * jnp.exp(zq - lse)).astype(BF)

    my_rows = gp_t.at[pl.ds(pl.multiple_of(c * 256, 256), 256), :]
    its_rows = gp_t.at[pl.ds(pl.multiple_of((1 - c) * 256, 256), 256), :]
    order = (2, 1, 3, 0)
    gcs = {}
    for j in order:
        cols = pl.ds(pl.multiple_of(lax.rem(y + j, 4) * 1024, 1024), 1024)
        give[:, cols] = dot(its_rows[...], q[:, cols]).astype(BF)
        gcs[j] = send(give.at[:, cols], got.at[:, cols], gc_s.at[j], gc_r.at[j], peer)
        gcs[j].start()
        kept[:, cols] = dot(my_rows[...], q[:, cols])

    def g1y(j):
        cols = pl.ds(pl.multiple_of(lax.rem(y + j, 4) * 1024, 1024), 1024)
        return cols, send(merged.at[:, cols], first_y.at[j - 1], g1_s.at[j], g1_r.at[j], ys[j])

    def g1x(j):
        there = xs[j]
        rows = pl.ds(pl.multiple_of(there["xh"] * 128, 128), 128)
        cols = pl.ds(pl.multiple_of(there["xl"] * 2048, 2048), 2048)
        return rows, cols, send(
            merged.at[rows, cols], first_x.at[j - 1], g1_s.at[j], g1_r.at[j], xs[j]
        )

    def g2(j, device):
        return send(second_out.at[j - 1], second_in.at[j - 1], g2_s.at[j], g2_r.at[j], device)

    @pl.when(c == 0)
    def _():
        for j in order[:3]:
            gcs[j].wait_recv()
            cols, copy = g1y(j)
            merged[:, cols] = (kept[:, cols] + got[:, cols].astype(F32)).astype(BF)
            copy.start()
        gcs[0].wait_recv()

    @pl.when(c == 1)
    def _():
        for j in order:
            gcs[j].wait_recv()
        for j in order[:3]:
            rows, cols, copy = g1x(j)
            merged[rows, cols] = (kept[rows, cols] + got[rows, cols].astype(F32)).astype(BF)
            copy.start()

    outs = []
    for i in range(PARTS):
        cols = pl.ds(i * CW, CW)
        value = dot(gp[:, :256], pa[0, :, cols]) + dot(gp[:, 256:], pa[1, :, cols])
        value = value + dot(gq[...], bank(0, at_s, i))
        t[:, cols] = (value * SCALE).astype(BF)
        outs.append(pltpu.make_async_copy(t.at[:, cols], qg_hbm.at[:, cols], out_sem.at[i]))
        outs[-1].start()

    @pl.when(c == 0)
    def _():
        for j in order[:3]:
            g1y(j)[1].wait_recv()
        for j in order:
            device = along_x(j)
            rows = pl.ds(pl.multiple_of(device["xh"] * 128, 128), 128)
            low = device["xl"] * 512
            cols = pl.ds(pl.multiple_of(y * 1024 + low, 512), 512)
            inner = pl.ds(pl.multiple_of(low, 512), 512)
            value = kept[rows, cols] + got[rows, cols].astype(F32)
            for k in range(3):
                value = value + first_y[k, rows, inner].astype(F32)
            if j:
                second_out[j - 1] = value.astype(BF)
                g2(j, device).start()
            else:
                piece[...] = value

    @pl.when(c == 1)
    def _():
        for j in order[:3]:
            g1x(j)[2].wait_recv()
        rows = pl.ds(pl.multiple_of(xh * 128, 128), 128)
        for j in order:
            low = lax.rem(y + j, 4) * 512
            cols = pl.ds(pl.multiple_of(xl * 2048 + low, 512), 512)
            inner = pl.ds(pl.multiple_of(low, 512), 512)
            value = kept[rows, cols] + got[rows, cols].astype(F32)
            for k in range(3):
                value = value + first_x[k, :, inner].astype(F32)
            if j:
                second_out[j - 1] = value.astype(BF)
                g2(j, ys[j]).start()
            else:
                piece[...] = value

    for j in order[:3]:
        g2(j, peer).wait_recv()
    piece[...] = piece[...] + (
        second_in[0].astype(F32) + second_in[1].astype(F32) + second_in[2].astype(F32)
    )

    def g3(j):
        rows = pl.ds(pl.multiple_of(lax.rem(z + j, 8) * 16, 16), 16)
        return send(piece.at[rows, :], third_in.at[j - 1], g3_s.at[j], g3_r.at[j], zs[j])

    for j in (4, 3, 5, 2, 6, 1, 7):
        g3(j).start()
    final = piece[pl.ds(pl.multiple_of(z * 16, 16), 16), :]
    for j in (1, 7, 2, 6, 3, 5, 4):
        g3(j).wait_recv()
        final = final + third_in[j - 1]
    col = (1 - c) * (y * 1024 + xl * 512) + c * (xl * 2048 + y * 512)
    part = pg_ref.at[:, pl.ds(pl.multiple_of(col, 512), 512)]
    part[...] = final * SCALE
    g4 = {j: send(part, part, g4_s.at[j], g4_r.at[j], dps[j]) for j in dps}
    for j in g4:
        g4[j].start()

    for j in pz:
        pz[j].wait_send()
    for copies in (px, py, gcs):
        for j in copies:
            copies[j].wait_send()
    pc.wait_send()

    def sent(s, carry):
        ring(s).wait_send()
        return carry

    lax.fori_loop(0, S - L, sent, 0)

    def shared(b, carry):
        share(b).wait_send()
        return carry

    lax.fori_loop(0, NB, shared, 0)

    @pl.when(rung)
    def _():
        def crossed(s, carry):
            cross(s).wait_send()
            return carry

        lax.fori_loop(0, N + L, crossed, 0)

    @pl.when(c == 0)
    def _():
        for j in order[:3]:
            g1y(j)[1].wait_send()

    @pl.when(c == 1)
    def _():
        for j in order[:3]:
            g1x(j)[2].wait_send()

    for j in order[:3]:
        g2(j, peer).wait_send()
    for j in zs:
        g3(j).wait_send()
    for copy in outs:
        copy.wait()
    for j in g4:
        g4[j].wait()


def body(queries, teacher_queries, passages, bank_student, bank_teacher, owner, positives, keep):
    hbm = pl.BlockSpec(memory_space=pl.ANY)
    vmem = pl.BlockSpec(memory_space=pltpu.VMEM)
    dma = pltpu.SemaphoreType.DMA
    loss, query_grad, passage_grad = pl.pallas_call(
        kernel,
        out_shape=(
            jax.ShapeDtypeStruct((1, 512), F32),
            jax.ShapeDtypeStruct((512, E), BF),
            jax.ShapeDtypeStruct((16, E), F32),
        ),
        in_specs=[pl.BlockSpec(memory_space=pltpu.SMEM), hbm, hbm, hbm, hbm, hbm, vmem, vmem],
        out_specs=(vmem, hbm, vmem),
        scratch_shapes=[
            pltpu.VMEM((512, E), BF),
            pltpu.VMEM((512, E), BF),
            pltpu.VMEM((2, 256, E), BF),
            pltpu.VMEM((PARTS, 256, CW), BF),
            pltpu.VMEM((PARTS, 256, CW), BF),
            pltpu.VMEM((S - L, 16, CW), BF),
            pltpu.VMEM((N + L, 16, CW), BF),
            pltpu.VMEM((2, S, 16, CW), BF),
            pltpu.VMEM((512, 512), F32),
            pltpu.VMEM((256, 512), F32),
            pltpu.VMEM((256, 512), F32),
            pltpu.VMEM((512, 512), BF),
            pltpu.VMEM((512, 512), BF),
            pltpu.VMEM((512, 256), BF),
            pltpu.VMEM((256, E), BF),
            pltpu.VMEM((256, E), BF),
            pltpu.VMEM((256, E), F32),
            pltpu.VMEM((256, E), BF),
            pltpu.VMEM((3, 256, 1024), BF),
            pltpu.VMEM((3, 128, 2048), BF),
            pltpu.VMEM((3, 128, 512), BF),
            pltpu.VMEM((3, 128, 512), BF),
            pltpu.VMEM((128, 512), F32),
            pltpu.VMEM((7, 16, 512), F32),
            dma((3,)), dma((PARTS,)), dma((PARTS,)), dma((PARTS,)),
            dma((S - L,)), dma((S - L,)), dma((N + L,)), dma((N + L,)), dma((NB,)), dma((NB,)),
            dma((8,)), dma((8,)), dma((4,)), dma((4,)), dma((4,)), dma((4,)), dma, dma,
            dma((4,)), dma((4,)), dma((4,)), dma((4,)), dma((4,)), dma((4,)),
            dma((8,)), dma((8,)), dma((8,)), dma((8,)), dma((PARTS,)),
        ],
        compiler_params=pltpu.CompilerParams(
            collective_id=0, has_side_effects=True, vmem_limit_bytes=60 << 20
        ),
        name="distill_step",
    )(
        owner, queries, teacher_queries, passages, bank_student, bank_teacher,
        positives.reshape(1, 512), keep,
    )
    return loss.reshape(512), query_grad, passage_grad


def solution(mesh):
    torus = Mesh(mesh.devices.reshape(8, 2, 2, 4, 2), AXES)
    in_specs = (
        P(AXES, None),
        P(AXES, None),
        P(WIDE, None),
        P(WIDE, None),
        P(WIDE, None),
        P(DP),
        P(AXES),
        P(AXES, None),
    )
    out_specs = (P(AXES), P(AXES, None), P(WIDE, None))
    return jax.shard_map(body, mesh=torus, in_specs=in_specs, out_specs=out_specs, check_vma=False)
```

time: 469 us -> 126 us (0.27)
  waiting for transfers between devices: 404 us -> 0 us
  Pallas kernels: 0 us -> 118 us
  matrix products: 19.4 us -> 0 us
  between operations: 16 us -> 1.29 us
  blocking collectives: 7.73 us -> 0 us
  starting transfers between devices: 6.26 us -> 0 us
    psum x1 -> x0, waiting for transfers between devices: 241 us -> none  [broadcast(): return lax.psum(block, axis)]
    pallas_call x0 -> x1, Pallas kernels: none -> 118 us  [body(): pl.pallas_call(kernel, out_shape=(jax.ShapeDtypeStruct((1, 512), F32), ja...]
    reduce_scatter x3 -> x0, waiting for transfers between devices: 103 us -> none  [own_block(): tiles = lax.psum_scatter(tiles, axes[k], scatter_dimension=0, tiled=True)]
    all_gather x2 -> x0, waiting for transfers between devices: 41.1 us -> none  [all_blocks(): tiles = lax.all_gather(tiles, axes[k])]
    dot_general x6 -> x0, matrix products: 19.4 us -> none  [the longest x1 4.82 us: body(): jnp.dot(grad_p, passage_store, preferred_element_type=jnp.float32)]
    all_to_all x1 -> x0, waiting for transfers between devices: 18.6 us -> none  [from_everyone(): return lax.all_to_all(copies, axis, split_axis=0, concat_axis=0, tiled=True)]
    all_gather x1 -> x0, blocking collectives: 7.73 us -> none  [all_blocks(): tiles = lax.all_gather(tiles, axes[k])]
    all_to_all x1 -> x0, starting transfers between devices: 6.01 us -> none  [from_everyone(): return lax.all_to_all(copies, axis, split_axis=0, concat_axis=0, tiled=True)]
  transfers between devices with their start and end apart: 7 -> 0, of which waited for: 6 -> 0; matrix products, arithmetic and copies ran while one was open for 4% -> 0% of each run, Pallas kernels for 0% -> 0%
where the time goes in v2:
time: 126 us; the launch traced here: 125 us
  Pallas kernels  118 us (94%)
  local copies, waits for them, and re-layouts  6.69 us (5%)
  between operations  1.29 us (1%)
    pallas_call x1, Pallas kernels, body(): pl.pallas_call(kernel, out_shape=(jax.ShapeDtypeStruct((1, 512), F32), ja...  118 us
    unnamed x5, local copies, waits for them, and re-layouts  6.69 us

profile of v2, /device:TPU:4, one launch (start us, length us, event | category | flops | bytes accessed | tf_op | source)
XLA Modules:
  0.0 125.5 jit_solution(8935403572341922356)
XLA Ops:
  1.3 117.5 %distill_step.1 = (f32[1,512]{1,0:T(1,128)}, bf16[512,4096]{1,0:T(8,128)(2,1)}, f32[16,4096]{1,0:T(8,128)}) custom-call(s32[1]{0:T(128)S(6)} %copy.14.owner_ref, bf16[512,4096]{1,0:T(8,128)(2,1)} %q_hbm.1, bf16[512,4096]{1,0:T(8,128)(2,1)} %t_hbm.1, bf16[16,4096]{1,0:T(8,128)(2,1)} %p_hbm.1, bf16[256,4096]{1,0:T(8,128)(2,1)} %bs_hbm.1, ...), custom_call_target="tpu_custom_call" | custom-call | tf_op jit(solution)/shard_map/distill_step/pallas_call | solution.py:439
  118.8 1.2 copy.15
  120.0 0.0 copy-start
  120.0 4.7 %copy.16 = bf16[512,4096]{1,0:T(8,128)(2,1)} copy(bf16[512,4096]{1,0:T(8,128)(2,1)} %get-tuple-element.13) | data formatting | bytes 8388608
  124.8 0.0 copy-done
  124.8 0.7 copy.17
Async XLA Ops:
  120.0 4.7 %copy-start = (f32[16,4096]{1,0:T(8,128)S(1)}, f32[16,4096]{1,0:T(8,128)}, u32[]{:S(2)}) copy-start(f32[16,4096]{1,0:T(8,128)} %get-tuple-element.14) | copy-start | bytes 786436

commit v3 on v2

--- a/solution.py
+++ b/solution.py
@@ -20,7 +20,7 @@
 PARTS = 4
 CW = E // PARTS
 N = PARTS * 16
-L = 8
+L = 9
 L2 = 12
 S = N + 8 * L + L2
 BATCH = 4
@@ -40,11 +40,11 @@
 
 
 def kernel(
-    owner_ref, q_hbm, t_hbm, p_hbm, bs_hbm, bt_hbm, pos_ref, keep_ref,
+    owner_ref, q_hbm, t_hbm, p_hbm, bs_hbm, bt_hbm, pos_ref, keep_hbm,
     loss_ref, qg_hbm, pg_ref,
-    q, t, pa, own, oth, ring_in, rung_in, stream,
+    q, t, keep_ref, pa, own, oth, ring_in, rung_in, stream,
     zp_t, zq_t, tt_t, gp_t, gp, gq,
-    give, got, kept, merged, first_y, first_x, second_out, second_in, piece, third_in,
+    give, got, kept, merged, first_y, first_x, second_out, second_in, piece, third_out, third_in,
     load_sem, own_sem, oth_s, oth_r, ring_s, ring_r, rung_s, rung_r, share_s, share_r,
     pz_s, pz_r, px_s, px_r, py_s, py_r, pc_s, pc_r,
     gc_s, gc_r, g1_s, g1_r, g2_s, g2_r, g3_s, g3_r, g4_s, g4_r, out_sem,
@@ -107,6 +107,7 @@
 
     load_q = pltpu.make_async_copy(q_hbm, q, load_sem.at[0])
     load_t = pltpu.make_async_copy(t_hbm, t, load_sem.at[1])
+    load_keep = pltpu.make_async_copy(keep_hbm, keep_ref, load_sem.at[3])
     pl.semaphore_wait(barrier, len(greeted))
 
     @pl.when(c == 0)
@@ -219,6 +220,7 @@
     run(0, 24)
     load_q.start()
     load_t.start()
+    load_keep.start()
     for j in pz:
         pz[j].wait_recv()
     for j in px:
@@ -235,6 +237,7 @@
     run(116, S)
     load_q.wait()
     load_t.wait()
+    load_keep.wait()
     pc.wait_recv()
 
     for h in range(2):
@@ -266,7 +269,9 @@
     k = lax.broadcasted_iota(jnp.int32, (512, 512), 0)
     ids = (lax.rem(k // 16, 8) * 4 + lax.rem(k // 128, 2) * 2 + k // 256) * 16 + lax.rem(k, 16)
     hit = (ids == pos_ref[...]).astype(F32)
-    loss_ref[...] = lse - jnp.sum(zp * hit, axis=0, keepdims=True)
+    loss = lse - jnp.sum(zp * hit, axis=0, keepdims=True)
+    for i in range(4):
+        loss_ref[pl.ds(i, 1), :] = loss[:, i * 128 : (i + 1) * 128]
     grad = jnp.exp(zp - lse) - hit
     gp_t[...] = grad.astype(BF)
     gp[...] = jnp.transpose(grad).astype(BF)
@@ -275,13 +280,17 @@
     my_rows = gp_t.at[pl.ds(pl.multiple_of(c * 256, 256), 256), :]
     its_rows = gp_t.at[pl.ds(pl.multiple_of((1 - c) * 256, 256), 256), :]
     order = (2, 1, 3, 0)
-    gcs = {}
-    for j in order:
-        cols = pl.ds(pl.multiple_of(lax.rem(y + j, 4) * 1024, 1024), 1024)
-        give[:, cols] = dot(its_rows[...], q[:, cols]).astype(BF)
-        gcs[j] = send(give.at[:, cols], got.at[:, cols], gc_s.at[j], gc_r.at[j], peer)
-        gcs[j].start()
-        kept[:, cols] = dot(my_rows[...], q[:, cols])
+    y_cols = [lax.rem(y + j, 4) * 1024 for j in order]
+    x_cols = [((1 - xl) * 2 + i) * 1024 for i in range(2)] + [(xl * 2 + i) * 1024 for i in range(2)]
+    gcs = []
+    for i in range(4):
+        for_it = pl.multiple_of(c * y_cols[i] + (1 - c) * x_cols[i], 1024)
+        for_me = pl.multiple_of((1 - c) * y_cols[i] + c * x_cols[i], 1024)
+        give[:, pl.ds(for_it, 1024)] = dot(its_rows[...], q[:, pl.ds(for_it, 1024)]).astype(BF)
+        there = give.at[:, pl.ds(for_it, 1024)]
+        gcs.append(send(there, got.at[:, pl.ds(for_it, 1024)], gc_s.at[i], gc_r.at[i], peer))
+        gcs[-1].start()
+        kept[:, pl.ds(for_me, 1024)] = dot(my_rows[...], q[:, pl.ds(for_me, 1024)])
 
     def g1y(j):
         cols = pl.ds(pl.multiple_of(lax.rem(y + j, 4) * 1024, 1024), 1024)
@@ -300,18 +309,19 @@
 
     @pl.when(c == 0)
     def _():
-        for j in order[:3]:
-            gcs[j].wait_recv()
+        for i, j in enumerate(order[:3]):
+            gcs[i].wait_recv()
             cols, copy = g1y(j)
             merged[:, cols] = (kept[:, cols] + got[:, cols].astype(F32)).astype(BF)
             copy.start()
-        gcs[0].wait_recv()
+        gcs[3].wait_recv()
 
     @pl.when(c == 1)
     def _():
-        for j in order:
-            gcs[j].wait_recv()
-        for j in order[:3]:
+        for j in (1, 3, 2):
+            if j != 3:
+                for i in (0, 1) if j == 1 else (2, 3):
+                    gcs[i].wait_recv()
             rows, cols, copy = g1x(j)
             merged[rows, cols] = (kept[rows, cols] + got[rows, cols].astype(F32)).astype(BF)
             copy.start()
@@ -324,6 +334,35 @@
         t[:, cols] = (value * SCALE).astype(BF)
         outs.append(pltpu.make_async_copy(t.at[:, cols], qg_hbm.at[:, cols], out_sem.at[i]))
         outs[-1].start()
+
+    for j in pz:
+        pz[j].wait_send()
+    for copies in (px, py):
+        for j in copies:
+            copies[j].wait_send()
+    pc.wait_send()
+    for copy in gcs:
+        copy.wait_send()
+
+    def sent(s, carry):
+        ring(s).wait_send()
+        return carry
+
+    lax.fori_loop(0, S - L, sent, 0)
+
+    def shared(b, carry):
+        share(b).wait_send()
+        return carry
+
+    lax.fori_loop(0, NB, shared, 0)
+
+    @pl.when(rung)
+    def _():
+        def crossed(s, carry):
+            cross(s).wait_send()
+            return carry
+
+        lax.fori_loop(0, N + L, crossed, 0)
 
     @pl.when(c == 0)
     def _():
@@ -368,49 +407,24 @@
         second_in[0].astype(F32) + second_in[1].astype(F32) + second_in[2].astype(F32)
     )
 
+    third_out[...] = piece[...].astype(BF)
+
     def g3(j):
         rows = pl.ds(pl.multiple_of(lax.rem(z + j, 8) * 16, 16), 16)
-        return send(piece.at[rows, :], third_in.at[j - 1], g3_s.at[j], g3_r.at[j], zs[j])
+        return send(third_out.at[rows, :], third_in.at[j - 1], g3_s.at[j], g3_r.at[j], zs[j])
 
     for j in (4, 3, 5, 2, 6, 1, 7):
         g3(j).start()
     final = piece[pl.ds(pl.multiple_of(z * 16, 16), 16), :]
     for j in (1, 7, 2, 6, 3, 5, 4):
         g3(j).wait_recv()
-        final = final + third_in[j - 1]
+        final = final + third_in[j - 1].astype(F32)
     col = (1 - c) * (y * 1024 + xl * 512) + c * (xl * 2048 + y * 512)
     part = pg_ref.at[:, pl.ds(pl.multiple_of(col, 512), 512)]
     part[...] = final * SCALE
     g4 = {j: send(part, part, g4_s.at[j], g4_r.at[j], dps[j]) for j in dps}
     for j in g4:
         g4[j].start()
-
-    for j in pz:
-        pz[j].wait_send()
-    for copies in (px, py, gcs):
-        for j in copies:
-            copies[j].wait_send()
-    pc.wait_send()
-
-    def sent(s, carry):
-        ring(s).wait_send()
-        return carry
-
-    lax.fori_loop(0, S - L, sent, 0)
-
-    def shared(b, carry):
-        share(b).wait_send()
-        return carry
-
-    lax.fori_loop(0, NB, shared, 0)
-
-    @pl.when(rung)
-    def _():
-        def crossed(s, carry):
-            cross(s).wait_send()
-            return carry
-
-        lax.fori_loop(0, N + L, crossed, 0)
 
     @pl.when(c == 0)
     def _():
@@ -439,15 +453,16 @@
     loss, query_grad, passage_grad = pl.pallas_call(
         kernel,
         out_shape=(
-            jax.ShapeDtypeStruct((1, 512), F32),
+            jax.ShapeDtypeStruct((4, 128), F32),
             jax.ShapeDtypeStruct((512, E), BF),
             jax.ShapeDtypeStruct((16, E), F32),
         ),
-        in_specs=[pl.BlockSpec(memory_space=pltpu.SMEM), hbm, hbm, hbm, hbm, hbm, vmem, vmem],
+        in_specs=[pl.BlockSpec(memory_space=pltpu.SMEM), hbm, hbm, hbm, hbm, hbm, vmem, hbm],
         out_specs=(vmem, hbm, vmem),
         scratch_shapes=[
             pltpu.VMEM((512, E), BF),
             pltpu.VMEM((512, E), BF),
+            pltpu.VMEM((512, 256), jnp.int32),
             pltpu.VMEM((2, 256, E), BF),
             pltpu.VMEM((PARTS, 256, CW), BF),
             pltpu.VMEM((PARTS, 256, CW), BF),
@@ -469,8 +484,9 @@
             pltpu.VMEM((3, 128, 512), BF),
             pltpu.VMEM((3, 128, 512), BF),
             pltpu.VMEM((128, 512), F32),
-            pltpu.VMEM((7, 16, 512), F32),
-            dma((3,)), dma((PARTS,)), dma((PARTS,)), dma((PARTS,)),
+            pltpu.VMEM((128, 512), BF),
+            pltpu.VMEM((7, 16, 512), BF),
+            dma((4,)), dma((PARTS,)), dma((PARTS,)), dma((PARTS,)),
             dma((S - L,)), dma((S - L,)), dma((N + L,)), dma((N + L,)), dma((NB,)), dma((NB,)),
             dma((8,)), dma((8,)), dma((4,)), dma((4,)), dma((4,)), dma((4,)), dma, dma,
             dma((4,)), dma((4,)), dma((4,)), dma((4,)), dma((4,)), dma((4,)),

time: 126 us -> 121 us (0.960)
  Pallas kernels: 118 us -> 113 us
    pallas_call x1, Pallas kernels: 118 us -> 113 us  [body(): pl.pallas_call(kernel, out_shape=(jax.ShapeDtypeStruct((4, 128), F32), ja...]
where the time goes in v3:
time: 121 us
  Pallas kernels  113 us (93%)
  local copies, waits for them, and re-layouts  6.69 us (6%)
  between operations  1.29 us (1%)
    pallas_call x1, Pallas kernels, body(): pl.pallas_call(kernel, out_shape=(jax.ShapeDtypeStruct((4, 128), F32), ja...  113 us
    unnamed x5, local copies, waits for them, and re-layouts  6.69 us

profile of v3, /device:TPU:4, one launch (start us, length us, event | category | flops | bytes accessed | tf_op | source)
XLA Modules:
  0.0 121.1 jit_solution(4370895794967798406)
XLA Ops:
  1.3 113.2 %distill_step.1 = (f32[4,128]{1,0:T(4,128)}, bf16[512,4096]{1,0:T(8,128)(2,1)}, f32[16,4096]{1,0:T(8,128)}) custom-call(s32[1]{0:T(128)S(6)} %copy.14.owner_ref, bf16[512,4096]{1,0:T(8,128)(2,1)} %q_hbm.1, bf16[512,4096]{1,0:T(8,128)(2,1)} %t_hbm.1, bf16[16,4096]{1,0:T(8,128)(2,1)} %p_hbm.1, bf16[256,4096]{1,0:T(8,128)(2,1)} %bs_hbm.1, ...), custom_call_target="tpu_custom_call" | custom-call | tf_op jit(solution)/shard_map/distill_step/pallas_call | solution.py:453
  114.4 1.2 %copy.15 = f32[512]{0:T(512)} copy(f32[512]{0:T(512)} %bitcast.2) | data formatting | bytes 4096
  115.7 0.0 copy-start
  115.7 4.7 %copy.16 = bf16[512,4096]{1,0:T(8,128)(2,1)} copy(bf16[512,4096]{1,0:T(8,128)(2,1)} %get-tuple-element.13) | data formatting | bytes 8388608
  120.4 0.0 copy-done
  120.4 0.7 copy.17
Async XLA Ops:
  115.7 4.7 %copy-start = (f32[16,4096]{1,0:T(8,128)S(1)}, f32[16,4096]{1,0:T(8,128)}, u32[]{:S(2)}) copy-start(f32[16,4096]{1,0:T(8,128)} %get-tuple-element.14) | copy-start | bytes 786436

commit v4 on v3

--- a/solution.py
+++ b/solution.py
@@ -19,14 +19,16 @@
 
 PARTS = 4
 CW = E // PARTS
-N = PARTS * 16
-L = 9
+PIECES = PARTS + 1
+ONE_WAY = 16 * (PARTS - 1)
+N = 16 * PIECES
+L = 8
 L2 = 12
-S = N + 8 * L + L2
+S = max(ONE_WAY + 8 * L, N + 4 * L) + L2
 BATCH = 4
 NB = S // BATCH
 assert S % BATCH == 0
-EDGES = sorted({0, L, L2, N, N + L, N + L + L2, S - L, S} | {16 * i for i in range(PARTS)})
+EDGES = sorted({0, L, L2, N, N + L, N + L + L2, S - L, S} | {16 * i for i in range(PIECES)})
 
 NT = (((1,), (1,)), ((), ()))
 
@@ -83,16 +85,20 @@
     load_p = pltpu.make_async_copy(p_hbm.at[:, pl.ds(pcol, 512)], mine_p, load_sem.at[2])
     load_p.start()
 
-    def own_loads(src):
+    def pieces(bank):
+        last = PARTS - 1
+        return [(bank, i) for i in range(last)] + [(bs_hbm, last), (bt_hbm, last)]
+
+    def own_loads(bank):
         return [
-            pltpu.make_async_copy(src.at[:, pl.ds(i * CW, CW)], own.at[i], own_sem.at[i])
-            for i in range(PARTS)
+            pltpu.make_async_copy(src.at[:, pl.ds(i * CW, CW)], own.at[k], own_sem.at[k])
+            for k, (src, i) in enumerate(pieces(bank))
         ]
 
-    def other_loads(src):
+    def other_loads(bank):
         return [
-            send(src.at[:, pl.ds(i * CW, CW)], oth.at[i], oth_s.at[i], oth_r.at[i], peer)
-            for i in range(PARTS)
+            send(src.at[:, pl.ds(i * CW, CW)], oth.at[k], oth_s.at[k], oth_r.at[k], peer)
+            for k, (src, i) in enumerate(pieces(bank))
         ]
 
     @pl.when(c == 0)
@@ -230,11 +236,11 @@
         px[j].wait_recv()
     for j in py:
         py[j].start()
-    run(40, 116)
+    run(40, 104)
     for j in py:
         py[j].wait_recv()
     pc.start()
-    run(116, S)
+    run(104, S)
     load_q.wait()
     load_t.wait()
     load_keep.wait()
@@ -248,15 +254,20 @@
         return carry
 
     lax.fori_loop(0, NB, got_share, 0)
-    _, _, at_s = place(0)
-    _, _, at_t = place(1)
-
-    def bank(core, at, i):
-        return stream[core, pl.ds(at + 16 * i, 16)].reshape(256, CW)
-
-    for target, core, at, left in ((zq_t, 0, at_s, q), (tt_t, 1, at_t, t)):
+    at = [place(0)[2], place(1)[2]]
+    nearer = jnp.where(at[0] <= at[1], 0, 1)
+    at_last = jnp.minimum(at[0], at[1]) + ONE_WAY
+
+    def bank(array, i):
+        if i < PARTS - 1:
+            rows = stream[array, pl.ds(at[array] + 16 * i, 16)]
+        else:
+            rows = stream[nearer, pl.ds(at_last + 16 * array, 16)]
+        return rows.reshape(256, CW)
+
+    for target, array, left in ((zq_t, 0, q), (tt_t, 1, t)):
         for i in range(PARTS):
-            part = dot_nt(bank(core, at, i), left[:, pl.ds(i * CW, CW)])
+            part = dot_nt(bank(array, i), left[:, pl.ds(i * CW, CW)])
             target[...] = part if i == 0 else target[...] + part
     zq = zq_t[...] * SCALE
     weight = jnp.transpose(keep_ref[...].astype(F32)) * jax.nn.sigmoid(-(tt_t[...] * SCALE))
@@ -330,7 +341,7 @@
     for i in range(PARTS):
         cols = pl.ds(i * CW, CW)
         value = dot(gp[:, :256], pa[0, :, cols]) + dot(gp[:, 256:], pa[1, :, cols])
-        value = value + dot(gq[...], bank(0, at_s, i))
+        value = value + dot(gq[...], bank(0, i))
         t[:, cols] = (value * SCALE).astype(BF)
         outs.append(pltpu.make_async_copy(t.at[:, cols], qg_hbm.at[:, cols], out_sem.at[i]))
         outs[-1].start()
@@ -464,8 +475,8 @@
             pltpu.VMEM((512, E), BF),
             pltpu.VMEM((512, 256), jnp.int32),
             pltpu.VMEM((2, 256, E), BF),
-            pltpu.VMEM((PARTS, 256, CW), BF),
-            pltpu.VMEM((PARTS, 256, CW), BF),
+            pltpu.VMEM((PIECES, 256, CW), BF),
+            pltpu.VMEM((PIECES, 256, CW), BF),
             pltpu.VMEM((S - L, 16, CW), BF),
             pltpu.VMEM((N + L, 16, CW), BF),
             pltpu.VMEM((2, S, 16, CW), BF),
@@ -486,7 +497,7 @@
             pltpu.VMEM((128, 512), F32),
             pltpu.VMEM((128, 512), BF),
             pltpu.VMEM((7, 16, 512), BF),
-            dma((4,)), dma((PARTS,)), dma((PARTS,)), dma((PARTS,)),
+            dma((4,)), dma((PIECES,)), dma((PIECES,)), dma((PIECES,)),
             dma((S - L,)), dma((S - L,)), dma((N + L,)), dma((N + L,)), dma((NB,)), dma((NB,)),
             dma((8,)), dma((8,)), dma((4,)), dma((4,)), dma((4,)), dma((4,)), dma, dma,
             dma((4,)), dma((4,)), dma((4,)), dma((4,)), dma((4,)), dma((4,)),

time: 121 us -> 116 us (0.959)
  Pallas kernels: 113 us -> 107 us
    pallas_call x1, Pallas kernels: 113 us -> 107 us  [body(): pl.pallas_call(kernel, out_shape=(jax.ShapeDtypeStruct((4, 128), F32), ja...]
where the time goes in v4:
time: 116 us; the launch traced here: 115 us
  Pallas kernels  107 us (92%)
  local copies, waits for them, and re-layouts  6.69 us (6%)
  between operations  1.29 us (1%)
    pallas_call x1, Pallas kernels, body(): pl.pallas_call(kernel, out_shape=(jax.ShapeDtypeStruct((4, 128), F32), ja...  107 us
    unnamed x5, local copies, waits for them, and re-layouts  6.69 us

profile of v4, /device:TPU:4, one launch (start us, length us, event | category | flops | bytes accessed | tf_op | source)
XLA Modules:
  0.0 115.5 jit_solution(16896170995101722132)
XLA Ops:
  1.3 107.5 %distill_step.1 = (f32[4,128]{1,0:T(4,128)}, bf16[512,4096]{1,0:T(8,128)(2,1)}, f32[16,4096]{1,0:T(8,128)}) custom-call(s32[1]{0:T(128)S(6)} %copy.14.owner_ref, bf16[512,4096]{1,0:T(8,128)(2,1)} %q_hbm.1, bf16[512,4096]{1,0:T(8,128)(2,1)} %t_hbm.1, bf16[16,4096]{1,0:T(8,128)(2,1)} %p_hbm.1, bf16[256,4096]{1,0:T(8,128)(2,1)} %bs_hbm.1, ...), custom_call_target="tpu_custom_call" | custom-call | tf_op jit(solution)/shard_map/distill_step/pallas_call | solution.py:464
  108.8 1.2 %copy.15 = f32[512]{0:T(512)} copy(f32[512]{0:T(512)} %bitcast.2) | data formatting | bytes 4096
  110.0 0.0 copy-start
  110.0 4.7 %copy.16 = bf16[512,4096]{1,0:T(8,128)(2,1)} copy(bf16[512,4096]{1,0:T(8,128)(2,1)} %get-tuple-element.13) | data formatting | bytes 8388608
  114.8 0.0 copy-done
  114.8 0.7 copy.17
Async XLA Ops:
  110.0 4.7 %copy-start = (f32[16,4096]{1,0:T(8,128)S(1)}, f32[16,4096]{1,0:T(8,128)}, u32[]{:S(2)}) copy-start(f32[16,4096]{1,0:T(8,128)} %get-tuple-element.14) | copy-start | bytes 786436
